TPU v7x, 32 devices: a whole 2x2x4 slice. The times are simulated.
32 devices in a mesh: img: 4 (over x, core), tok: 8 (over z, y).
Axes of the slice: x: 2, y: 2, z: 4, core: 2. Of those that a mesh axis runs over, the one named last changes fastest.
Arguments:
- student: bfloat16 [4, 1024, 4096], P('img', None, 'tok'), may hold values from -0.32 to 0.32
- teacher: bfloat16 [4, 64, 64, 4096], P('img', None, None, 'tok'), may hold values from -160 to 160
Outputs:
- gradient: bfloat16 [4, 1024, 4096], P('img', None, 'tok')
- loss: float32 [], replicated
All inputs are finite; a program needn't handle non-finite values.
Results may differ from a plain program's by a relative error of at most 0.0069.
Values may be sent and summed in bfloat16 or wider, within the bound.
A program may use at most 64 MiB of HBM per device.

v0:
```python
import jax
import jax.numpy as jnp
from jax import lax
from jax.sharding import PartitionSpec as P

cubic_taps = (-0.09375, 0.59375, 0.59375, -0.09375)
epsilon = 1e-06


def shrink(padded, length, dimension):
    weighted = [
        cubic_taps[offset]
        * lax.slice_in_dim(padded, offset, offset + 2 * length - 1, 2, dimension).astype(
            jnp.float32
        )
        for offset in range(4)
    ]
    return weighted[0] + weighted[1] + weighted[2] + weighted[3]


def inner_rows(left_rows, right_rows):
    return lax.dot_general(
        left_rows, right_rows, (((1,), (1,)), ((), ())), preferred_element_type=jnp.float32
    )


def per_device(student, teacher):
    tokens_all = student.shape[1]
    features = student[0].astype(jnp.float32)
    local_teacher = teacher[0]
    padded = jnp.pad(local_teacher, ((1, 1), (1, 1), (0, 0)), mode="edge")
    vertical = shrink(padded, local_teacher.shape[0] // 2, 0)
    shrunk = shrink(vertical, local_teacher.shape[1] // 2, 1).reshape(
        tokens_all, local_teacher.shape[2]
    )
    student_sums, teacher_sums = lax.psum(
        (jnp.sum(features * features, axis=1), jnp.sum(shrunk * shrunk, axis=1)), "tok"
    )
    inverse = lax.rsqrt(student_sums + epsilon)[:, None]
    unit_rows = features * inverse
    unit_low = unit_rows.astype(jnp.bfloat16)
    teacher_unit = (shrunk * lax.rsqrt(teacher_sums + epsilon)[:, None]).astype(jnp.bfloat16)
    mismatch = lax.psum_scatter(
        inner_rows(unit_low, unit_low) - inner_rows(teacher_unit, teacher_unit),
        "tok",
        scatter_dimension=0,
        tiled=True,
    )
    squared = jnp.sum(mismatch * mismatch)
    mismatch_low = mismatch.astype(jnp.bfloat16)
    pull_grad = 4.0 * jnp.dot(
        lax.all_gather(mismatch_low, "tok", axis=0, tiled=True),
        unit_low,
        preferred_element_type=jnp.float32,
    )
    along = lax.psum(jnp.sum(unit_rows * pull_grad, axis=1), "tok")
    gradient = inverse * pull_grad - inverse * unit_rows * along[:, None]
    total_loss = lax.psum(squared, ("img", "tok")) / tokens_all
    return (gradient.astype(jnp.bfloat16)[None], total_loss)


def solution(mesh):
    return jax.shard_map(
        per_device,
        mesh=mesh,
        in_specs=(P("img", None, "tok"), P("img", None, None, "tok")),
        out_specs=(P("img", None, "tok"), P()),
        check_vma=False,
    )
```

profile of v0, /device:TPU:0, one launch (start us, length us, event | category | flops | bytes accessed | tf_op | source)
XLA Modules:
  0.0 263.8 jit_solution(3681172191667079634)
XLA Ops:
  7.2 0.0 reduce-scatter.2.cloned.1.call-start
  7.2 0.9 slice_bitcast_fusion.1
  8.1 6.5 %fusion.9 = bf16[66,66,512]{2,1,0:T(8,128)(2,1)S(1)} fusion(bf16[1,64,512]{2,1,0:T(8,128)(2,1)S(1)} %get-tuple-element.9, bf16[64,64,512]{2,1,0:T(8,128)(2,1)} %bitcast.42, bf16[1,64,512]{2,1,0:T(8,128)(2,1)S(1)} %get-tuple-element.8), kind=kLoop, calls=%fused_computation.11 | loop fusion | flops 57987072 | bytes 8785920 | tf_op jit(solution)/shard_map/jit(_pad)/concatenate | solution.py:31
  14.6 3.1 %multiply_add_fusion = f32[32,66,512]{2,1,0:T(8,128)} fusion(bf16[66,66,512]{2,1,0:T(8,128)(2,1)S(1)} %fusion.9), kind=kLoop, calls=%fused_computation.14 | loop fusion | flops 11894784 | bytes 12976128 | tf_op jit(solution)/shard_map/add | solution.py:18
  17.7 9.8 %slice.56 = f32[32,32,512]{2,1,0:T(8,128)} slice(f32[32,66,512]{2,1,0:T(8,128)} %multiply_add_fusion), slice={[0:32:1], [0:63:2], [0:512:1]} | slice | bytes 4194304 | tf_op jit(solution)/shard_map/slice | solution.py:13
  27.5 9.8 %slice.57 = f32[32,32,512]{2,1,0:T(8,128)} slice(f32[32,66,512]{2,1,0:T(8,128)} %multiply_add_fusion), slice={[0:32:1], [1:64:2], [0:512:1]} | slice | bytes 4194304 | tf_op jit(solution)/shard_map/slice | solution.py:13
  37.3 9.9 %slice.58 = f32[32,32,512]{2,1,0:T(8,128)} slice(f32[32,66,512]{2,1,0:T(8,128)} %multiply_add_fusion), slice={[0:32:1], [2:65:2], [0:512:1]} | slice | bytes 4194304 | tf_op jit(solution)/shard_map/slice | solution.py:13
  47.2 10.0 %slice.59 = f32[32,32,512]{2,1,0:T(8,128)} slice(f32[32,66,512]{2,1,0:T(8,128)} %multiply_add_fusion), slice={[0:32:1], [3:66:2], [0:512:1]} | slice | bytes 4194304 | tf_op jit(solution)/shard_map/slice | solution.py:13
  57.2 4.1 %multiply_reduce_fusion = (f32[32,32]{1,0:T(8,128)S(1)}, f32[32,32,512]{2,1,0:T(8,128)S(1)}) fusion(f32[32,32,512]{2,1,0:T(8,128)} %slice.59, f32[32,32,512]{2,1,0:T(8,128)} %slice.58, f32[32,32,512]{2,1,0:T(8,128)} %slice.57, f32[32,32,512]{2,1,0:T(8,128)} %slice.56), kind=kLoop, calls=%fused_computation.30 | loop fusion | flops 4717568 | bytes 10489856 | tf_op jit(solution)/shard_map/reduce_sum | solution.py:37
  61.3 0.1 reduce_sum.40
  61.4 1.5 copy.4
  62.9 0.2 fusion.21
  63.1 23.4 %all-reduce = (f32[1024]{0:T(1024)S(1)}, f32[1024]{0:T(1024)S(1)}) all-reduce(f32[1024]{0:T(1024)S(1)} %fusion.21, f32[1024]{0:T(1024)S(1)} %reduce_sum.40), channel_id=1, replica_groups=mesh['img'=4,'tok'=8] {'tok'}, use_global_device_ids=true, to_apply=%region_1.2 | all-reduce | flops 2048 | bytes 16384 | tf_op jit(solution)/shard_map/psum | solution.py:36
  86.6 0.1 mul.107
  86.6 1.3 fusion.24
  87.9 0.2 multiply_convert_fusion
  88.2 3.2 %convolution_subtract_fusion = f32[1024,1024]{1,0:T(8,128)} fusion(f32[1024,1024]{1,0:T(8,128)S(1)} %fusion.24, bf16[1024,512]{1,0:T(8,128)(2,1)S(1)} %bitcast.41), kind=kOutput, calls=%fused_computation.22 | convolution fusion | flops 1074790400 | bytes 9437184 | tf_op jit(solution)/shard_map/dot_general | solution.py:22
  91.4 0.0 reduce-scatter.2.cloned.1.call-update
  91.4 0.0 all-gather.2.cloned.1.call-start
  91.4 85.7 %reduce-scatter.2.cloned.1.call-done = f32[128,1024]{1,0:T(8,128)} async-done(((f32[1024,1024]{1,0:T(8,128)}), f32[128,1024]{1,0:T(8,128)}) %reduce-scatter.2.cloned.1.call-update) | async-done | bytes 524304 | tf_op jit(solution)/shard_map/reduce_scatter | solution.py:43
  177.1 2.6 multiply_reduce_fusion.1
  179.7 0.0 all-gather.2.cloned.1.call-update
  179.7 41.9 %psum.31 = f32[]{:T(128)} all-reduce(f32[]{:T(128)} %get-tuple-element.10), channel_id=1, replica_groups=mesh['img'=4,'tok'=8] {'img','tok'}, use_global_device_ids=true, to_apply=%region_8.9 | all-reduce | flops 1 | bytes 8 | tf_op jit(solution)/shard_map/psum | solution.py:58
  222.2 7.3 %all-gather.2.cloned.1.call-done = bf16[1024,1024]{1,0:T(8,128)(2,1)} async-done(((bf16[128,1024]{1,0:T(8,128)(2,1)}), bf16[1024,1024]{1,0:T(8,128)(2,1)}) %all-gather.2.cloned.1.call-update) | async-done | bytes 2097168 | tf_op jit(solution)/shard_map/all_gather | solution.py:52
  229.5 4.2 %fusion.20 = (f32[1024]{0:T(1024)S(1)}, f32[1024,512]{0,1:T(8,128)}) fusion(bf16[1,1024,512]{1,2,0:T(8,128)(2,1)S(1)} %copy.4, f32[1024]{0:T(1024)S(1)} %get-tuple-element.13, bf16[1024,1024]{1,0:T(8,128)(2,1)} %all-gather.2.cloned.1.call-done), kind=kOutput, calls=%fused_computation.26 | convolution fusion | flops 1077935104 | bytes 5251072 | tf_op jit(solution)/shard_map/dot_general | solution.py:51
  233.7 18.7 %psum.30 = f32[1024]{0:T(1024)S(1)} all-reduce(f32[1024]{0:T(1024)S(1)} %get-tuple-element.14), channel_id=1, replica_groups=mesh['img'=4,'tok'=8] {'tok'}, use_global_device_ids=true, to_apply=%region_6.7 | all-reduce | flops 1024 | bytes 8192 | tf_op jit(solution)/shard_map/psum | solution.py:56
  252.4 2.1 fusion.26
  254.5 1.3 copy.5
  (1 shorter events, 0.0 us)
Async XLA Ops:
  7.2 169.9 %reduce-scatter.2.cloned.1.call-start = ((), (), s32[]{:S(2)}) async-start(), calls=%async_computation.1 | async-start | bytes 4718592 | tf_op jit(solution)/shard_map/reduce_scatter | solution.py:43
  91.4 138.1 %all-gather.2.cloned.1.call-start = ((), (), s32[]{:S(2)}) async-start(), calls=%async_computation.2 | async-start | bytes 2359296 | tf_op jit(solution)/shard_map/all_gather | solution.py:52
Sparse Core Ops, SparseCore 0:
  91.5 85.5 reduce-scatter.1
  179.8 49.6 all-gather.1
where the time goes:
time: 265 us; the launch traced here: 264 us
  waiting for transfers between devices  93 us (35%)
  blocking collectives  84 us (32%)
  local copies, waits for them, and re-layouts  43.3 us (16%)
  other arithmetic  18.8 us (7%)
  between operations  15.9 us (6%)
  matrix products  8.71 us (3%)
    reduce_scatter x1, waiting for transfers between devices, per_device(): lax.psum_scatter(inner_rows(unit_low, unit_low) - inner_rows(teacher_unit...  85.7 us
    psum x1, blocking collectives, per_device(): total_loss = lax.psum(squared, ('img', 'tok')) / tokens_all  41.9 us
    slice x4, local copies, waits for them, and re-layouts, shrink(): lax.slice_in_dim(padded, offset, offset + 2 * length - 1, 2, dimension)  39.5 us
    psum x1, blocking collectives, per_device(): lax.psum((jnp.sum(features * features, axis=1), jnp.sum(shrunk * shrunk,...  23.4 us
    psum x1, blocking collectives, per_device(): along = lax.psum(jnp.sum(unit_rows * pull_grad, axis=1), 'tok')  18.7 us
    all_gather x1, waiting for transfers between devices, per_device(): lax.all_gather(mismatch_low, 'tok', axis=0, tiled=True)  7.29 us
    concatenate x1, other arithmetic, per_device(): padded = jnp.pad(local_teacher, ((1, 1), (1, 1), (0, 0)), mode='edge')  6.47 us
  transfers between devices with their start and end apart: 2, of which 2 were waited for; matrix products, arithmetic and copies ran while one was open for 0% of the time, Pallas kernels for 0%

commit v1 on v0

v1 whole, which is shorter than its diff:
```python
import functools

import jax
import jax.numpy as jnp
from jax import lax
from jax.experimental import pallas as pl
from jax.experimental.pallas import tpu as pltpu
from jax.sharding import PartitionSpec as P

cubic_taps = (-0.09375, 0.59375, 0.59375, -0.09375)
epsilon = 1e-06
LANES = 128
BLOCK = 256
LAG = 1


def lane_tiles_sum(x):
    total = x[:, :LANES]
    for start in range(LANES, x.shape[1], LANES):
        total = total + x[:, start : start + LANES]
    return total


def spread(column, width):
    return jnp.concatenate([column] * (width // LANES), axis=1)


def kernel(
    sizes, student_hbm, teacher_hbm, taps_ref, out_ref, loss_ref,
    sbuf, tbuf, hbuf, shrunk, unit_low, teach_low, part, inv, tinv,
    snorm, tnorm, along, losses, img_losses,
    own, ysend, yrecv, zin, zout, mlow, pull, sqacc,
    load_sem, s_send, s_recv, t_send, t_recv, a_send, a_recv, l_send, l_recv,
    i_send, i_recv, y_send, y_recv, z_send, z_recv, g_send, g_recv,
):
    n, m = sizes
    tokens, feats = unit_low.shape
    height, width = tbuf.shape[0], tbuf.shape[1]
    group = load_sem.shape[0] - 1
    rows_per = height // group
    half_w = width // 2
    nb = tokens // BLOCK
    tiles = tokens // LANES
    me = lax.axis_index("tok")
    img = lax.axis_index("img")
    col = lax.rem(me, 2)
    row = me // 2
    chain = n // 2
    pairs = [(i, j) for i in range(nb) for j in range(i, nb)]
    count = len(pairs) // 2
    early = jnp.where(row < (chain + 1) // 2, 0, 1)
    late = 1 - early
    rank = jnp.minimum(row, chain - 1 - row)

    def load(g):
        rows = pl.ds(g * rows_per, rows_per)
        return pltpu.make_async_copy(
            teacher_hbm.at[0, rows], tbuf.at[rows], load_sem.at[g]
        )

    student_load = pltpu.make_async_copy(student_hbm.at[0], sbuf, load_sem.at[group])
    student_load.start()

    @pl.loop(0, group)
    def _(g):
        load(g).start()

    barrier = pltpu.get_barrier_semaphore()
    for p in range(1, n):
        pl.semaphore_signal(barrier, 1, device_id={"tok": lax.rem(me + p, n)})
    for p in range(1, m):
        pl.semaphore_signal(barrier, 1, device_id={"img": lax.rem(img + p, m)})

    def gather_copies(buf, send, recv, axis, here, size):
        return [
            pltpu.make_async_remote_copy(
                src_ref=buf.at[here],
                dst_ref=buf.at[here],
                send_sem=send.at[p - 1],
                recv_sem=recv.at[p - 1],
                device_id={axis: lax.rem(here + p, size)},
            )
            for p in range(1, size)
        ]

    def pack_rows(buf):
        @pl.loop(0, tiles)
        def _(b):
            block = part[pl.ds(pl.multiple_of(b * LANES, LANES), LANES), :]
            buf[me, pl.ds(b, 1), :] = jnp.sum(block.T, axis=0, keepdims=True)

    def summed(buf, size):
        total = buf[0]
        for k in range(1, size):
            total = total + buf[k]
        return total

    def unpack_rows(values, dst):
        for b in range(tiles):
            dst[b * LANES : (b + 1) * LANES, :] = jnp.broadcast_to(
                values[b : b + 1, :], (LANES, LANES)
            ).T

    def slab(b):
        return pl.ds(pl.multiple_of(b * LANES, LANES), LANES)

    @pl.when(rank == 0)
    def _():
        zin[early] = jnp.zeros(zin.shape[1:], zin.dtype)

    sqacc[...] = jnp.zeros_like(sqacc)
    student_load.wait()

    @pl.loop(0, tiles)
    def _(b):
        x = sbuf[slab(b), :].astype(jnp.float32)
        part[slab(b), :] = lane_tiles_sum(x * x)

    pack_rows(snorm)
    pl.semaphore_wait(barrier, n - 1 + m - 1)
    s_copies = gather_copies(snorm, s_send, s_recv, "tok", me, n)
    for copy in s_copies:
        copy.start()

    @pl.loop(0, group)
    def _(g):
        load(g).wait()
        x = tbuf[pl.ds(g * rows_per, rows_per)].reshape(rows_per * width, feats)
        y = jnp.dot(taps_ref[...], x, preferred_element_type=jnp.float32)
        hbuf[pl.ds(g * rows_per + 1, rows_per)] = y.reshape(rows_per, half_w, feats)

    hbuf[0] = hbuf[1]
    hbuf[height + 1] = hbuf[height]

    @pl.loop(0, height // 2)
    def _(a):
        v = cubic_taps[0] * hbuf[2 * a]
        for k in range(1, 4):
            v = v + cubic_taps[k] * hbuf[2 * a + k]
        rows = pl.ds(pl.multiple_of(a * half_w, half_w), half_w)
        shrunk[rows, :] = v
        part[rows, :] = lane_tiles_sum(v * v)

    pack_rows(tnorm)
    t_copies = gather_copies(tnorm, t_send, t_recv, "tok", me, n)
    for copy in t_copies:
        copy.start()

    for copy in s_copies:
        copy.wait_recv()
    unpack_rows(lax.rsqrt(summed(snorm, n) + epsilon), inv)

    @pl.loop(0, tiles)
    def _(b):
        x = sbuf[slab(b), :].astype(jnp.float32) * spread(inv[slab(b), :], feats)
        unit_low[slab(b), :] = x.astype(jnp.bfloat16)

    def pick(k, c):
        first, second = pairs[k], pairs[count + k]
        i = first[0] + c * (second[0] - first[0])
        j = first[1] + c * (second[1] - first[1])
        return i, j

    def strip(i):
        return pl.ds(pl.multiple_of(i * BLOCK, BLOCK), BLOCK)

    def gram(low, i, j):
        return lax.dot_general(
            low[strip(i), :], low[strip(j), :], (((1,), (1,)), ((), ())),
            preferred_element_type=jnp.float32,
        )

    for k in range(count):
        own[count + k] = gram(unit_low, *pick(k, 1 - col))
    for k in range(count):
        own[k] = gram(unit_low, *pick(k, col))

    for copy in t_copies:
        copy.wait_recv()
    unpack_rows(lax.rsqrt(summed(tnorm, n) + epsilon), tinv)

    @pl.loop(0, tiles)
    def _(b):
        x = shrunk[slab(b), :] * spread(tinv[slab(b), :], feats)
        teach_low[slab(b), :] = x.astype(jnp.bfloat16)

    y_copies = []
    for k in range(count):
        d = own[count + k] - gram(teach_low, *pick(k, 1 - col))
        ysend[k] = d.astype(jnp.bfloat16)
        copy = pltpu.make_async_remote_copy(
            src_ref=ysend.at[k], dst_ref=yrecv.at[k],
            send_sem=y_send.at[k], recv_sem=y_recv.at[k],
            device_id={"tok": me + 1 - 2 * col},
        )
        copy.start()
        y_copies.append(copy)
    for k in range(count):
        own[k] = own[k] - gram(teach_low, *pick(k, col))

    def chain_copy(direction, k):
        step = 2 - 4 * direction
        return pltpu.make_async_remote_copy(
            src_ref=zout.at[direction, k], dst_ref=zin.at[direction, k],
            send_sem=z_send.at[direction, k], recv_sem=z_recv.at[direction, k],
            device_id={"tok": lax.rem(me + step + n, n)},
        )

    def block_copy(k):
        i, j = pick(k, col)
        block = mlow.at[strip(i), strip(j)]
        return pltpu.make_async_remote_copy(
            src_ref=block, dst_ref=block,
            send_sem=g_send.at[k], recv_sem=g_recv.at[k],
            device_id={"tok": me + 1 - 2 * col},
        )

    def run_early(k):
        y_copies[k].wait_recv()
        mine = own[k] + yrecv[k].astype(jnp.float32)
        copy = chain_copy(early, k)

        @pl.when(rank > 0)
        def _():
            copy.wait_recv()

        total = mine + zin[early, k].astype(jnp.float32)
        zout[early, k] = total.astype(jnp.bfloat16)
        own[k] = mine
        own[count + k] = total
        copy.start()

    def run_late(k):
        copy = chain_copy(late, k)
        copy.wait_recv()
        incoming = zin[late, k].astype(jnp.float32)
        total = own[count + k] + incoming
        i, j = pick(k, col)
        low = total.astype(jnp.bfloat16)

        @pl.when(rank > 0)
        def _():
            zout[late, k] = (own[k] + incoming).astype(jnp.bfloat16)
            copy.start()

        mlow[strip(i), strip(j)] = low
        block_copy(k).start()
        weight = jnp.where(i == j, 1.0, 2.0)
        sqacc[...] += weight * jnp.sum(total * total, axis=0, keepdims=True)

        @pl.when(i != j)
        def _():
            mlow[strip(j), strip(i)] = total.T.astype(jnp.bfloat16)

    for t in range(count + LAG):
        if t < count:
            run_early(t)
        if t >= LAG:
            run_late(t - LAG)

    squared = jnp.sum(sqacc[...], axis=1, keepdims=True)
    losses[me] = jnp.broadcast_to(squared, losses.shape[1:])
    l_copies = gather_copies(losses, l_send, l_recv, "tok", me, n)
    for copy in l_copies:
        copy.start()

    for k in range(count):
        block_copy(k).wait_recv()
        i, j = pick(k, 1 - col)

        @pl.when(i != j)
        def _():
            block = mlow[strip(i), strip(j)].astype(jnp.float32)
            mlow[strip(j), strip(i)] = block.T.astype(jnp.bfloat16)

    @pl.loop(0, nb)
    def _(b):
        rows = strip(b)
        p = 4.0 * jnp.dot(mlow[rows, :], unit_low[...], preferred_element_type=jnp.float32)
        pull[rows, :] = p
        unit = sbuf[rows, :].astype(jnp.float32) * spread(inv[rows, :], feats)
        part[rows, :] = lane_tiles_sum(unit * p)

    pack_rows(along)
    a_copies = gather_copies(along, a_send, a_recv, "tok", me, n)
    for copy in a_copies:
        copy.start()

    for copy in l_copies:
        copy.wait_recv()
    img_losses[img] = summed(losses, n)
    i_copies = gather_copies(img_losses, i_send, i_recv, "img", img, m)
    for copy in i_copies:
        copy.start()

    for copy in a_copies:
        copy.wait_recv()
    unpack_rows(summed(along, n), tinv)

    @pl.loop(0, tiles)
    def _(b):
        scale = spread(inv[slab(b), :], feats)
        unit = sbuf[slab(b), :].astype(jnp.float32) * scale
        grad = scale * pull[slab(b), :] - scale * unit * spread(tinv[slab(b), :], feats)
        out_ref[0, slab(b), :] = grad.astype(out_ref.dtype)

    for copy in i_copies:
        copy.wait_recv()
    loss_ref[...] = summed(img_losses, m) / (chain * tokens)

    for copy in s_copies + t_copies + l_copies + a_copies + i_copies + y_copies:
        copy.wait_send()
    for k in range(count):
        block_copy(k).wait_send()
        chain_copy(early, k).wait_send()

        @pl.when(rank > 0)
        def _():
            chain_copy(late, k).wait_send()


def tap_matrix(width, rows_per):
    half = width // 2
    source = jnp.arange(width)[None, :]
    taps = jnp.zeros((half, width), jnp.float32)
    for q in range(4):
        wanted = jnp.clip(2 * jnp.arange(half)[:, None] - 1 + q, 0, width - 1)
        taps = taps + jnp.where(source == wanted, cubic_taps[q], 0.0)
    return jnp.kron(jnp.eye(rows_per, dtype=jnp.float32), taps).astype(jnp.bfloat16)


def per_device(n, m, student, teacher):
    _, tokens, feats = student.shape
    _, height, width, _ = teacher.shape
    rows_per = max(1, 256 // width)
    groups = height // rows_per
    nb = tokens // BLOCK
    count = nb * (nb + 1) // 4
    tiles = tokens // LANES
    f32, bf16 = jnp.float32, jnp.bfloat16
    vmem, dma = pltpu.VMEM, pltpu.SemaphoreType.DMA
    gradient, loss = pl.pallas_call(
        functools.partial(kernel, (n, m)),
        name="anchor",
        out_shape=(
            jax.ShapeDtypeStruct(student.shape, bf16),
            jax.ShapeDtypeStruct((8, LANES), f32),
        ),
        in_specs=[
            pl.BlockSpec(memory_space=pl.ANY),
            pl.BlockSpec(memory_space=pl.ANY),
            pl.BlockSpec(memory_space=pltpu.VMEM),
        ],
        out_specs=(
            pl.BlockSpec(memory_space=pltpu.VMEM),
            pl.BlockSpec(memory_space=pltpu.VMEM),
        ),
        scratch_shapes=[
            vmem((tokens, feats), bf16),
            vmem((height, width, feats), bf16),
            vmem((height + 2, width // 2, feats), f32),
            vmem((tokens, feats), f32),
            vmem((tokens, feats), bf16),
            vmem((tokens, feats), bf16),
            vmem((tokens, LANES), f32),
            vmem((tokens, LANES), f32),
            vmem((tokens, LANES), f32),
            vmem((n, tiles, LANES), f32),
            vmem((n, tiles, LANES), f32),
            vmem((n, tiles, LANES), f32),
            vmem((n, 8, LANES), f32),
            vmem((m, 8, LANES), f32),
            vmem((2 * count, BLOCK, BLOCK), f32),
            vmem((count, BLOCK, BLOCK), bf16),
            vmem((count, BLOCK, BLOCK), bf16),
            vmem((2, count, BLOCK, BLOCK), bf16),
            vmem((2, count, BLOCK, BLOCK), bf16),
            vmem((tokens, tokens), bf16),
            vmem((tokens, feats), f32),
            vmem((1, BLOCK), f32),
            dma((groups + 1,)),
            dma((n - 1,)), dma((n - 1,)), dma((n - 1,)), dma((n - 1,)),
            dma((n - 1,)), dma((n - 1,)), dma((n - 1,)), dma((n - 1,)),
            dma((m - 1,)), dma((m - 1,)),
            dma((count,)), dma((count,)),
            dma((2, count)), dma((2, count)),
            dma((count,)), dma((count,)),
        ],
        compiler_params=pltpu.CompilerParams(
            collective_id=0, has_side_effects=True, vmem_limit_bytes=56 * 1024 * 1024
        ),
    )(student, teacher, tap_matrix(width, rows_per))
    return gradient, loss[0, 0]


def solution(mesh):
    return jax.shard_map(
        functools.partial(per_device, mesh.shape["tok"], mesh.shape["img"]),
        mesh=mesh,
        in_specs=(P("img", None, "tok"), P("img", None, None, "tok")),
        out_specs=(P("img", None, "tok"), P()),
        check_vma=False,
    )
```

time: 265 us -> 84.3 us (0.32)
  waiting for transfers between devices: 93 us -> 0 us
  blocking collectives: 84 us -> 0 us
  Pallas kernels: 0 us -> 78.9 us
  local copies, waits for them, and re-layouts: 43.3 us -> 4.22 us
  other arithmetic: 18.8 us -> 0.22 us
  between operations: 15.9 us -> 0.67 us
  matrix products: 8.71 us -> 0 us
    reduce_scatter x1 -> x0, waiting for transfers between devices: 85.7 us -> none  [per_device(): lax.psum_scatter(inner_rows(unit_low, unit_low) - inner_rows(teacher_unit...]
    psum x3 -> x0, blocking collectives: 84 us -> none  [the longest x1 41.9 us: per_device(): total_loss = lax.psum(squared, ('img', 'tok')) / tokens_all]
    pallas_call x0 -> x1, Pallas kernels: none -> 78.9 us  [per_device(): pl.pallas_call(functools.partial(kernel, (n, m)), name='anchor', out_shap...]
    slice x5 -> x1, local copies, waits for them, and re-layouts: 40.4 us -> 1.19 us  [per_device(): return (gradient, loss[0, 0])]
    dot_general x3 -> x0, matrix products: 8.71 us -> none  [the longest x2 4.53 us: inner_rows(): lax.dot_general(left_rows, right_rows, (((1,), (1,)), ((), ())), preferre...]
    all_gather x1 -> x0, waiting for transfers between devices: 7.29 us -> none  [per_device(): lax.all_gather(mismatch_low, 'tok', axis=0, tiled=True)]
    reduce_sum x3 -> x0, other arithmetic: 6.95 us -> none  [the longest x1 4.14 us: per_device(): jnp.sum(shrunk * shrunk, axis=1)]
    concatenate x1 -> x0, other arithmetic: 6.47 us -> none  [per_device(): padded = jnp.pad(local_teacher, ((1, 1), (1, 1), (0, 0)), mode='edge')]
  transfers between devices with their start and end apart: 2 -> 0, of which waited for: 2 -> 0; matrix products, arithmetic and copies ran while one was open for 0% -> 0% of each run, Pallas kernels for 0% -> 0%
where the time goes in v1:
time: 84.3 us; the launch traced here: 84 us
  Pallas kernels  78.9 us (94%)
  local copies, waits for them, and re-layouts  4.22 us (5%)
    pallas_call x1, Pallas kernels, per_device(): pl.pallas_call(functools.partial(kernel, (n, m)), name='anchor', out_shap...  78.9 us
    unnamed x1, local copies, waits for them, and re-layouts  2.26 us

profile of v1, /device:TPU:0, one launch (start us, length us, event | category | flops | bytes accessed | tf_op | source)
XLA Modules:
  0.0 84.0 jit_solution(11283241850043571837)
XLA Ops:
  0.7 0.1 select_add_fusion
  0.8 0.1 multiply_convert_fusion
  0.9 0.8 convert_element_type.14.taps_ref
  1.6 78.9 %anchor.1 = (bf16[1,1024,512]{2,1,0:T(8,128)(2,1)}, f32[8,128]{1,0:T(8,128)}) custom-call(bf16[1,1024,512]{2,1,0:T(8,128)(2,1)} %student_hbm.1, bf16[1,64,64,512]{3,2,1,0:T(8,128)(2,1)} %teacher_hbm.1, bf16[128,256]{1,0:T(8,128)(2,1)} %convert_element_type.14.taps_ref), custom_call_target="tpu_custom_call" | custom-call | tf_op jit(solution)/shard_map/anchor/pallas_call | solution.py:342
  80.6 1.2 %slice.3 = f32[1,1]{1,0:T(1,128)} slice(f32[8,128]{1,0:T(8,128)} %get-tuple-element.5), slice={[0:1], [0:1]} | slice | bytes 8 | tf_op jit(solution)/shard_map/slice | solution.py:393
  81.8 2.3 %copy.5 = bf16[1,1024,512]{2,1,0:T(8,128)(2,1)} copy(bf16[1,1024,512]{2,1,0:T(8,128)(2,1)} %get-tuple-element.12) | data formatting | bytes 2097152
  (3 shorter events, 0.0 us)

commit v2 on v1

--- a/solution.py
+++ b/solution.py
@@ -2,6 +2,7 @@
 
 import jax
 import jax.numpy as jnp
+import numpy as np
 from jax import lax
 from jax.experimental import pallas as pl
 from jax.experimental.pallas import tpu as pltpu
@@ -11,7 +12,8 @@
 epsilon = 1e-06
 LANES = 128
 BLOCK = 256
-LAG = 1
+SPLIT = 2
+LAG = 2
 
 
 def lane_tiles_sum(x):
@@ -29,7 +31,7 @@
     sizes, student_hbm, teacher_hbm, taps_ref, out_ref, loss_ref,
     sbuf, tbuf, hbuf, shrunk, unit_low, teach_low, part, inv, tinv,
     snorm, tnorm, along, losses, img_losses,
-    own, ysend, yrecv, zin, zout, mlow, pull, sqacc,
+    own, prefix, theirs, ysend, yrecv, zin, zout, mlow, pull, sqacc,
     load_sem, s_send, s_recv, t_send, t_recv, a_send, a_recv, l_send, l_recv,
     i_send, i_recv, y_send, y_recv, z_send, z_recv, g_send, g_recv,
 ):
@@ -47,7 +49,9 @@
     row = me // 2
     chain = n // 2
     pairs = [(i, j) for i in range(nb) for j in range(i, nb)]
-    count = len(pairs) // 2
+    half = len(pairs) // 2
+    count = half * SPLIT
+    depth = BLOCK // SPLIT
     early = jnp.where(row < (chain + 1) // 2, 0, 1)
     late = 1 - early
     rank = jnp.minimum(row, chain - 1 - row)
@@ -117,17 +121,17 @@
         part[slab(b), :] = lane_tiles_sum(x * x)
 
     pack_rows(snorm)
-    pl.semaphore_wait(barrier, n - 1 + m - 1)
-    s_copies = gather_copies(snorm, s_send, s_recv, "tok", me, n)
-    for copy in s_copies:
-        copy.start()
-
     @pl.loop(0, group)
     def _(g):
         load(g).wait()
         x = tbuf[pl.ds(g * rows_per, rows_per)].reshape(rows_per * width, feats)
         y = jnp.dot(taps_ref[...], x, preferred_element_type=jnp.float32)
         hbuf[pl.ds(g * rows_per + 1, rows_per)] = y.reshape(rows_per, half_w, feats)
+
+    pl.semaphore_wait(barrier, n - 1 + m - 1)
+    s_copies = gather_copies(snorm, s_send, s_recv, "tok", me, n)
+    for copy in s_copies:
+        copy.start()
 
     hbuf[0] = hbuf[1]
     hbuf[height + 1] = hbuf[height]
@@ -156,7 +160,7 @@
         unit_low[slab(b), :] = x.astype(jnp.bfloat16)
 
     def pick(k, c):
-        first, second = pairs[k], pairs[count + k]
+        first, second = pairs[k], pairs[half + k]
         i = first[0] + c * (second[0] - first[0])
         j = first[1] + c * (second[1] - first[1])
         return i, j
@@ -170,10 +174,11 @@
             preferred_element_type=jnp.float32,
         )
 
-    for k in range(count):
-        own[count + k] = gram(unit_low, *pick(k, 1 - col))
-    for k in range(count):
-        own[k] = gram(unit_low, *pick(k, col))
+    for k in range(half):
+        theirs[k] = gram(unit_low, *pick(k, 1 - col))
+    for k in range(half):
+        pieces = gram(unit_low, *pick(k, col))
+        own[k * SPLIT : (k + 1) * SPLIT] = pieces.reshape(SPLIT, depth, BLOCK)
 
     for copy in t_copies:
         copy.wait_recv()
@@ -185,18 +190,21 @@
         teach_low[slab(b), :] = x.astype(jnp.bfloat16)
 
     y_copies = []
-    for k in range(count):
-        d = own[count + k] - gram(teach_low, *pick(k, 1 - col))
-        ysend[k] = d.astype(jnp.bfloat16)
-        copy = pltpu.make_async_remote_copy(
-            src_ref=ysend.at[k], dst_ref=yrecv.at[k],
-            send_sem=y_send.at[k], recv_sem=y_recv.at[k],
-            device_id={"tok": me + 1 - 2 * col},
-        )
-        copy.start()
-        y_copies.append(copy)
-    for k in range(count):
-        own[k] = own[k] - gram(teach_low, *pick(k, col))
+    for k in range(half):
+        d = theirs[k] - gram(teach_low, *pick(k, 1 - col))
+        pieces = d.astype(jnp.bfloat16).reshape(SPLIT, depth, BLOCK)
+        ysend[k * SPLIT : (k + 1) * SPLIT] = pieces
+        for t in range(k * SPLIT, (k + 1) * SPLIT):
+            copy = pltpu.make_async_remote_copy(
+                src_ref=ysend.at[t], dst_ref=yrecv.at[t],
+                send_sem=y_send.at[t], recv_sem=y_recv.at[t],
+                device_id={"tok": me + 1 - 2 * col},
+            )
+            copy.start()
+            y_copies.append(copy)
+    for k in range(half):
+        d = gram(teach_low, *pick(k, col)).reshape(SPLIT, depth, BLOCK)
+        own[k * SPLIT : (k + 1) * SPLIT] = own[k * SPLIT : (k + 1) * SPLIT] - d
 
     def chain_copy(direction, k):
         step = 2 - 4 * direction
@@ -206,9 +214,14 @@
             device_id={"tok": lax.rem(me + step + n, n)},
         )
 
+    def piece(k, c):
+        i, j = pick(k // SPLIT, c)
+        start = i * BLOCK + (k % SPLIT) * depth
+        return i, j, pl.ds(pl.multiple_of(start, depth), depth)
+
     def block_copy(k):
-        i, j = pick(k, col)
-        block = mlow.at[strip(i), strip(j)]
+        i, j, rows = piece(k, col)
+        block = mlow.at[rows, strip(j)]
         return pltpu.make_async_remote_copy(
             src_ref=block, dst_ref=block,
             send_sem=g_send.at[k], recv_sem=g_recv.at[k],
@@ -227,15 +240,15 @@
         total = mine + zin[early, k].astype(jnp.float32)
         zout[early, k] = total.astype(jnp.bfloat16)
         own[k] = mine
-        own[count + k] = total
+        prefix[k] = total
         copy.start()
 
     def run_late(k):
         copy = chain_copy(late, k)
         copy.wait_recv()
         incoming = zin[late, k].astype(jnp.float32)
-        total = own[count + k] + incoming
-        i, j = pick(k, col)
+        total = prefix[k] + incoming
+        i, j, rows = piece(k, col)
         low = total.astype(jnp.bfloat16)
 
         @pl.when(rank > 0)
@@ -243,20 +256,29 @@
             zout[late, k] = (own[k] + incoming).astype(jnp.bfloat16)
             copy.start()
 
-        mlow[strip(i), strip(j)] = low
+        mlow[rows, strip(j)] = low
         block_copy(k).start()
         weight = jnp.where(i == j, 1.0, 2.0)
         sqacc[...] += weight * jnp.sum(total * total, axis=0, keepdims=True)
 
         @pl.when(i != j)
         def _():
-            mlow[strip(j), strip(i)] = total.T.astype(jnp.bfloat16)
-
-    for t in range(count + LAG):
-        if t < count:
-            run_early(t)
-        if t >= LAG:
-            run_late(t - LAG)
+            mlow[strip(j), rows] = total.T.astype(jnp.bfloat16)
+
+    def run_chain(lag):
+        for t in range(count + lag):
+            if t < count:
+                run_early(t)
+            if t >= lag:
+                run_late(t - lag)
+
+    @pl.when(rank == 0)
+    def _():
+        run_chain(count)
+
+    @pl.when(rank > 0)
+    def _():
+        run_chain(min(LAG, count))
 
     squared = jnp.sum(sqacc[...], axis=1, keepdims=True)
     losses[me] = jnp.broadcast_to(squared, losses.shape[1:])
@@ -266,12 +288,12 @@
 
     for k in range(count):
         block_copy(k).wait_recv()
-        i, j = pick(k, 1 - col)
+        i, j, rows = piece(k, 1 - col)
 
         @pl.when(i != j)
         def _():
-            block = mlow[strip(i), strip(j)].astype(jnp.float32)
-            mlow[strip(j), strip(i)] = block.T.astype(jnp.bfloat16)
+            block = mlow[rows, strip(j)].astype(jnp.float32)
+            mlow[strip(j), rows] = block.T.astype(jnp.bfloat16)
 
     @pl.loop(0, nb)
     def _(b):
@@ -321,12 +343,11 @@
 
 def tap_matrix(width, rows_per):
     half = width // 2
-    source = jnp.arange(width)[None, :]
-    taps = jnp.zeros((half, width), jnp.float32)
-    for q in range(4):
-        wanted = jnp.clip(2 * jnp.arange(half)[:, None] - 1 + q, 0, width - 1)
-        taps = taps + jnp.where(source == wanted, cubic_taps[q], 0.0)
-    return jnp.kron(jnp.eye(rows_per, dtype=jnp.float32), taps).astype(jnp.bfloat16)
+    taps = np.zeros((half, width), np.float32)
+    for b in range(half):
+        for q in range(4):
+            taps[b, min(max(2 * b - 1 + q, 0), width - 1)] += cubic_taps[q]
+    return jnp.asarray(np.kron(np.eye(rows_per, dtype=np.float32), taps), jnp.bfloat16)
 
 
 def per_device(n, m, student, teacher):
@@ -335,7 +356,9 @@
     rows_per = max(1, 256 // width)
     groups = height // rows_per
     nb = tokens // BLOCK
-    count = nb * (nb + 1) // 4
+    half = nb * (nb + 1) // 4
+    count = half * SPLIT
+    depth = BLOCK // SPLIT
     tiles = tokens // LANES
     f32, bf16 = jnp.float32, jnp.bfloat16
     vmem, dma = pltpu.VMEM, pltpu.SemaphoreType.DMA
@@ -370,11 +393,13 @@
             vmem((n, tiles, LANES), f32),
             vmem((n, 8, LANES), f32),
             vmem((m, 8, LANES), f32),
-            vmem((2 * count, BLOCK, BLOCK), f32),
-            vmem((count, BLOCK, BLOCK), bf16),
-            vmem((count, BLOCK, BLOCK), bf16),
-            vmem((2, count, BLOCK, BLOCK), bf16),
-            vmem((2, count, BLOCK, BLOCK), bf16),
+            vmem((count, depth, BLOCK), f32),
+            vmem((count, depth, BLOCK), f32),
+            vmem((half, BLOCK, BLOCK), f32),
+            vmem((count, depth, BLOCK), bf16),
+            vmem((count, depth, BLOCK), bf16),
+            vmem((2, count, depth, BLOCK), bf16),
+            vmem((2, count, depth, BLOCK), bf16),
             vmem((tokens, tokens), bf16),
             vmem((tokens, feats), f32),
             vmem((1, BLOCK), f32),

time: 84.3 us -> 59 us (0.70)
  Pallas kernels: 78.9 us -> 54.6 us
    pallas_call x1, Pallas kernels: 78.9 us -> 54.6 us  [per_device(): pl.pallas_call(functools.partial(kernel, (n, m)), name='anchor', out_shap...]
where the time goes in v2:
time: 59 us; the launch traced here: 58.7 us
  Pallas kernels  54.6 us (93%)
  local copies, waits for them, and re-layouts  3.45 us (6%)
  between operations  0.64 us (1%)
    pallas_call x1, Pallas kernels, per_device(): pl.pallas_call(functools.partial(kernel, (n, m)), name='anchor', out_shap...  54.6 us
    unnamed x1, local copies, waits for them, and re-layouts  2.26 us
    slice x1, local copies, waits for them, and re-layouts, per_device(): return (gradient, loss[0, 0])  1.19 us

profile of v2, /device:TPU:0, one launch (start us, length us, event | category | flops | bytes accessed | tf_op | source)
XLA Modules:
  0.0 58.7 jit_solution(12270889601219142053)
XLA Ops:
  0.6 54.6 %anchor.1 = (bf16[1,1024,512]{2,1,0:T(8,128)(2,1)}, f32[8,128]{1,0:T(8,128)}) custom-call(bf16[1,1024,512]{2,1,0:T(8,128)(2,1)} %student_hbm.1, bf16[1,64,64,512]{3,2,1,0:T(8,128)(2,1)} %teacher_hbm.1, bf16[128,256]{1,0:T(8,128)(2,1)} %constant.2.clone.taps_ref), custom_call_target="tpu_custom_call" | custom-call | tf_op jit(solution)/shard_map/anchor/pallas_call | solution.py:365
  55.3 1.2 %slice.3 = f32[1,1]{1,0:T(1,128)} slice(f32[8,128]{1,0:T(8,128)} %get-tuple-element.5), slice={[0:1], [0:1]} | slice | bytes 8 | tf_op jit(solution)/shard_map/slice | solution.py:418
  56.5 2.3 %copy.6 = bf16[1,1024,512]{2,1,0:T(8,128)(2,1)} copy(bf16[1,1024,512]{2,1,0:T(8,128)(2,1)} %get-tuple-element.8) | data formatting | bytes 2097152

commit v3 on v2

--- a/solution.py
+++ b/solution.py
@@ -48,8 +48,11 @@
     col = lax.rem(me, 2)
     row = me // 2
     chain = n // 2
-    pairs = [(i, j) for i in range(nb) for j in range(i, nb)]
-    half = len(pairs) // 2
+    square = [(i, i) for i in range(nb)]
+    upper = [(i, j) for i in range(nb) for j in range(i + 1, nb)]
+    diag, off = len(square) // 2, len(upper) // 2
+    pairs = square[:diag] + upper[:off] + square[diag:] + upper[off:]
+    half = diag + off
     count = half * SPLIT
     depth = BLOCK // SPLIT
     early = jnp.where(row < (chain + 1) // 2, 0, 1)
@@ -189,6 +192,9 @@
         x = shrunk[slab(b), :] * spread(tinv[slab(b), :], feats)
         teach_low[slab(b), :] = x.astype(jnp.bfloat16)
 
+    def skip(k):
+        return (k % SPLIT) * depth if k < diag * SPLIT else 0
+
     y_copies = []
     for k in range(half):
         d = theirs[k] - gram(teach_low, *pick(k, 1 - col))
@@ -196,7 +202,7 @@
         ysend[k * SPLIT : (k + 1) * SPLIT] = pieces
         for t in range(k * SPLIT, (k + 1) * SPLIT):
             copy = pltpu.make_async_remote_copy(
-                src_ref=ysend.at[t], dst_ref=yrecv.at[t],
+                src_ref=ysend.at[t, :, skip(t) :], dst_ref=yrecv.at[t, :, skip(t) :],
                 send_sem=y_send.at[t], recv_sem=y_recv.at[t],
                 device_id={"tok": me + 1 - 2 * col},
             )
@@ -209,7 +215,8 @@
     def chain_copy(direction, k):
         step = 2 - 4 * direction
         return pltpu.make_async_remote_copy(
-            src_ref=zout.at[direction, k], dst_ref=zin.at[direction, k],
+            src_ref=zout.at[direction, k, :, skip(k) :],
+            dst_ref=zin.at[direction, k, :, skip(k) :],
             send_sem=z_send.at[direction, k], recv_sem=z_recv.at[direction, k],
             device_id={"tok": lax.rem(me + step + n, n)},
         )
@@ -217,11 +224,22 @@
     def piece(k, c):
         i, j = pick(k // SPLIT, c)
         start = i * BLOCK + (k % SPLIT) * depth
-        return i, j, pl.ds(pl.multiple_of(start, depth), depth)
+        columns = pl.ds(pl.multiple_of(j * BLOCK + skip(k), depth), BLOCK - skip(k))
+        return i, j, pl.ds(pl.multiple_of(start, depth), depth), columns
+
+    def mirror(k, c, block):
+        _, j, rows, _ = piece(k, c)
+        first = 0
+        if k < diag * SPLIT:
+            first = skip(k) + depth
+            block = block[:, depth:]
+        if first < BLOCK:
+            start = pl.multiple_of(j * BLOCK + first, depth)
+            mlow[pl.ds(start, BLOCK - first), rows] = block.T.astype(jnp.bfloat16)
 
     def block_copy(k):
-        i, j, rows = piece(k, col)
-        block = mlow.at[rows, strip(j)]
+        _, _, rows, columns = piece(k, col)
+        block = mlow.at[rows, columns]
         return pltpu.make_async_remote_copy(
             src_ref=block, dst_ref=block,
             send_sem=g_send.at[k], recv_sem=g_recv.at[k],
@@ -230,40 +248,44 @@
 
     def run_early(k):
         y_copies[k].wait_recv()
-        mine = own[k] + yrecv[k].astype(jnp.float32)
+        cut = skip(k)
+        mine = own[k, :, cut:] + yrecv[k, :, cut:].astype(jnp.float32)
         copy = chain_copy(early, k)
 
         @pl.when(rank > 0)
         def _():
             copy.wait_recv()
 
-        total = mine + zin[early, k].astype(jnp.float32)
-        zout[early, k] = total.astype(jnp.bfloat16)
-        own[k] = mine
-        prefix[k] = total
+        total = mine + zin[early, k, :, cut:].astype(jnp.float32)
+        zout[early, k, :, cut:] = total.astype(jnp.bfloat16)
+        own[k, :, cut:] = mine
+        prefix[k, :, cut:] = total
         copy.start()
 
     def run_late(k):
         copy = chain_copy(late, k)
         copy.wait_recv()
-        incoming = zin[late, k].astype(jnp.float32)
-        total = prefix[k] + incoming
-        i, j, rows = piece(k, col)
+        cut = skip(k)
+        incoming = zin[late, k, :, cut:].astype(jnp.float32)
+        total = prefix[k, :, cut:] + incoming
+        _, _, rows, columns = piece(k, col)
         low = total.astype(jnp.bfloat16)
 
         @pl.when(rank > 0)
         def _():
-            zout[late, k] = (own[k] + incoming).astype(jnp.bfloat16)
+            zout[late, k, :, cut:] = (own[k, :, cut:] + incoming).astype(jnp.bfloat16)
             copy.start()
 
-        mlow[rows, strip(j)] = low
+        mlow[rows, columns] = low
         block_copy(k).start()
-        weight = jnp.where(i == j, 1.0, 2.0)
-        sqacc[...] += weight * jnp.sum(total * total, axis=0, keepdims=True)
-
-        @pl.when(i != j)
-        def _():
-            mlow[strip(j), rows] = total.T.astype(jnp.bfloat16)
+        sums = jnp.sum(total * total, axis=0, keepdims=True)
+        if k < diag * SPLIT:
+            sqacc[:, :depth] += sums[:, :depth]
+            if cut + depth < BLOCK:
+                sqacc[:, cut + depth :] += 2.0 * sums[:, depth:]
+        else:
+            sqacc[...] += 2.0 * sums
+        mirror(k, col, total)
 
     def run_chain(lag):
         for t in range(count + lag):
@@ -288,12 +310,8 @@
 
     for k in range(count):
         block_copy(k).wait_recv()
-        i, j, rows = piece(k, 1 - col)
-
-        @pl.when(i != j)
-        def _():
-            block = mlow[rows, strip(j)].astype(jnp.float32)
-            mlow[strip(j), rows] = block.T.astype(jnp.bfloat16)
+        _, _, rows, columns = piece(k, 1 - col)
+        mirror(k, 1 - col, mlow[rows, columns].astype(jnp.float32))
 
     @pl.loop(0, nb)
     def _(b):
@@ -356,7 +374,7 @@
     rows_per = max(1, 256 // width)
     groups = height // rows_per
     nb = tokens // BLOCK
-    half = nb * (nb + 1) // 4
+    half = nb // 2 + nb * (nb - 1) // 4
     count = half * SPLIT
     depth = BLOCK // SPLIT
     tiles = tokens // LANES

time: 59 us -> 58.5 us (level)
  no operation moved by 1% of the time
where the time goes in v3:
time: 58.5 us; the launch traced here: 58.3 us
  Pallas kernels  54.2 us (93%)
  local copies, waits for them, and re-layouts  3.45 us (6%)
  between operations  0.64 us (1%)
    pallas_call x1, Pallas kernels, per_device(): pl.pallas_call(functools.partial(kernel, (n, m)), name='anchor', out_shap...  54.2 us
    unnamed x1, local copies, waits for them, and re-layouts  2.26 us
    slice x1, local copies, waits for them, and re-layouts, per_device(): return (gradient, loss[0, 0])  1.19 us

profile of v3, /device:TPU:0, one launch (start us, length us, event | category | flops | bytes accessed | tf_op | source)
XLA Modules:
  0.0 58.3 jit_solution(2252804449034394304)
XLA Ops:
  0.6 54.2 %anchor.1 = (bf16[1,1024,512]{2,1,0:T(8,128)(2,1)}, f32[8,128]{1,0:T(8,128)}) custom-call(bf16[1,1024,512]{2,1,0:T(8,128)(2,1)} %student_hbm.1, bf16[1,64,64,512]{3,2,1,0:T(8,128)(2,1)} %teacher_hbm.1, bf16[128,256]{1,0:T(8,128)(2,1)} %constant.2.clone.taps_ref), custom_call_target="tpu_custom_call" | custom-call | tf_op jit(solution)/shard_map/anchor/pallas_call | solution.py:383
  54.8 1.2 %slice.3 = f32[1,1]{1,0:T(1,128)} slice(f32[8,128]{1,0:T(8,128)} %get-tuple-element.5), slice={[0:1], [0:1]} | slice | bytes 8 | tf_op jit(solution)/shard_map/slice | solution.py:436
  56.0 2.3 %copy.6 = bf16[1,1024,512]{2,1,0:T(8,128)(2,1)} copy(bf16[1,1024,512]{2,1,0:T(8,128)(2,1)} %get-tuple-element.8) | data formatting | bytes 2097152

commit v4 on v3

--- a/solution.py
+++ b/solution.py
@@ -51,7 +51,7 @@
     square = [(i, i) for i in range(nb)]
     upper = [(i, j) for i in range(nb) for j in range(i + 1, nb)]
     diag, off = len(square) // 2, len(upper) // 2
-    pairs = square[:diag] + upper[:off] + square[diag:] + upper[off:]
+    pairs = upper[:off] + square[:diag] + upper[off:] + square[diag:]
     half = diag + off
     count = half * SPLIT
     depth = BLOCK // SPLIT
@@ -193,7 +193,7 @@
         teach_low[slab(b), :] = x.astype(jnp.bfloat16)
 
     def skip(k):
-        return (k % SPLIT) * depth if k < diag * SPLIT else 0
+        return (k % SPLIT) * depth if k >= off * SPLIT else 0
 
     y_copies = []
     for k in range(half):
@@ -230,7 +230,7 @@
     def mirror(k, c, block):
         _, j, rows, _ = piece(k, c)
         first = 0
-        if k < diag * SPLIT:
+        if k >= off * SPLIT:
             first = skip(k) + depth
             block = block[:, depth:]
         if first < BLOCK:
@@ -279,7 +279,7 @@
         mlow[rows, columns] = low
         block_copy(k).start()
         sums = jnp.sum(total * total, axis=0, keepdims=True)
-        if k < diag * SPLIT:
+        if k >= off * SPLIT:
             sqacc[:, :depth] += sums[:, :depth]
             if cut + depth < BLOCK:
                 sqacc[:, cut + depth :] += 2.0 * sums[:, depth:]

time: 58.5 us -> 58.1 us (level)
  no operation moved by 1% of the time
where the time goes in v4:
time: 58.1 us; the launch traced here: 57.9 us
  Pallas kernels  53.8 us (93%)
  local copies, waits for them, and re-layouts  3.45 us (6%)
  between operations  0.64 us (1%)
    pallas_call x1, Pallas kernels, per_device(): pl.pallas_call(functools.partial(kernel, (n, m)), name='anchor', out_shap...  53.8 us
    unnamed x1, local copies, waits for them, and re-layouts  2.26 us
    slice x1, local copies, waits for them, and re-layouts, per_device(): return (gradient, loss[0, 0])  1.19 us

profile of v4, /device:TPU:0, one launch (start us, length us, event | category | flops | bytes accessed | tf_op | source)
XLA Modules:
  0.0 57.9 jit_solution(9911401601273216804)
XLA Ops:
  0.6 53.8 %anchor.1 = (bf16[1,1024,512]{2,1,0:T(8,128)(2,1)}, f32[8,128]{1,0:T(8,128)}) custom-call(bf16[1,1024,512]{2,1,0:T(8,128)(2,1)} %student_hbm.1, bf16[1,64,64,512]{3,2,1,0:T(8,128)(2,1)} %teacher_hbm.1, bf16[128,256]{1,0:T(8,128)(2,1)} %constant.2.clone.taps_ref), custom_call_target="tpu_custom_call" | custom-call | tf_op jit(solution)/shard_map/anchor/pallas_call | solution.py:383
  54.4 1.2 %slice.3 = f32[1,1]{1,0:T(1,128)} slice(f32[8,128]{1,0:T(8,128)} %get-tuple-element.5), slice={[0:1], [0:1]} | slice | bytes 8 | tf_op jit(solution)/shard_map/slice | solution.py:436
  55.6 2.3 %copy.6 = bf16[1,1024,512]{2,1,0:T(8,128)(2,1)} copy(bf16[1,1024,512]{2,1,0:T(8,128)(2,1)} %get-tuple-element.8) | data formatting | bytes 2097152
